TPU v7x, 32 devices: a whole 2x2x4 slice. The times are simulated.
32 devices in a mesh: day: 2 (over x), row: 16 (over z, y, core).
Axes of the slice: x: 2, y: 2, z: 4, core: 2. Of those that a mesh axis runs over, the one named last changes fastest.
Arguments:
- spectra: bfloat16 [4096, 2, 2, 4096], P(('day', 'row')), parts along dimension 0, may hold values from -110 to 110
- pair_channels: int32 [64, 128, 2], P('row'), may hold values from 0 to 2047, as said below
- pair_live: int32 [64, 128], P('row'), may hold values from 0 to 1, as said below
Outputs:
- correlations: float32 [128, 128, 512], P(('day', 'row')), parts along dimension 0
There are 2 independent parts, one for each index of `day`. A program takes and returns all parts, laid end to end along the dimension named above; an argument that names none is the same for every part. Nothing has to cross between parts.
Inputs may be any that keep to these rules, and one draw needn't show every extreme that they name: `pair_channels`: pair slots of device i of row are tiles i * 4 to (i + 1) * 4 - 1; their first channels are that device's own channels i * 128 to (i + 1) * 128 - 1, and their second channels lie within 128 channels of the first; distances of exactly 128 occur on both sides. `pair_live`: in each device's pair slots (tile by tile, pair by pair) the live slots come first and the padding after; every device has 128 live slots or more, and one device's slots are all live.
All inputs are finite; a program needn't handle non-finite values.
Results may differ from a plain program's by a relative error of at most 0.003.
Values may be sent and summed in bfloat16 or wider, within the bound.
A program may use at most 192 MiB of HBM per device.

v0:
```python
import math
import jax
import jax.numpy as jnp
from jax import lax
from jax.sharding import PartitionSpec as P

WIN = 2
FREQ = 4096
BAND = 64
LAGS = 512
HALO = 128


def padded(block, sides, width):
    for axis, dim in sides:
        count = lax.axis_size(axis)
        forward = [(i, i + 1) for i in range(count - 1)]
        backward = [(target, source) for source, target in forward]
        low = lax.ppermute(
            lax.slice_in_dim(block, block.shape[dim] - width, None, axis=dim), axis, forward
        )
        high = lax.ppermute(lax.slice_in_dim(block, 0, width, axis=dim), axis, backward)
        block = jnp.concatenate([low, block, high], axis=dim)
    return block


def build_table(bin_total, lag_total):
    bin_index = jnp.arange(bin_total, dtype=jnp.int32)[:, None]
    shifts = jnp.arange(lag_total, dtype=jnp.int32)[None, :] - lag_total // 2
    phase_int = jnp.mod(bin_index * shifts, 2 * bin_total)
    angle_rad = phase_int.astype(jnp.float32) * (math.pi / bin_total)
    return jnp.concatenate([jnp.cos(angle_rad), -jnp.sin(angle_rad)], axis=0).astype(jnp.bfloat16)


def whiten(raw_rows, common):
    removed = raw_rows.astype(jnp.float32) - common[None]
    magnitude = jnp.sqrt(removed[:, :, 0] ** 2 + removed[:, :, 1] ** 2)
    row_count, window_count, bin_count = magnitude.shape
    banded = magnitude.reshape(row_count, window_count, bin_count // BAND, BAND)
    band_level = jnp.mean(banded, axis=3, keepdims=True) + 1e-06
    scaled = (
        removed.reshape(row_count, window_count, 2, bin_count // BAND, BAND)
        / band_level[:, :, None]
    )
    return scaled.reshape(raw_rows.shape).astype(jnp.bfloat16)


def cross_rows(first_rows, second_rows):
    first_f32 = first_rows.astype(jnp.float32)
    second_f32 = second_rows.astype(jnp.float32)
    real_part = jnp.sum(
        first_f32[:, :, 0] * second_f32[:, :, 0] + first_f32[:, :, 1] * second_f32[:, :, 1], axis=1
    )
    imag_part = jnp.sum(
        first_f32[:, :, 1] * second_f32[:, :, 0] - first_f32[:, :, 0] * second_f32[:, :, 1], axis=1
    )
    return jnp.concatenate([real_part, imag_part], axis=1).astype(jnp.bfloat16)


def body(spectra, pair_channels, pair_live):
    own_rows = spectra.shape[0]
    channels = own_rows * lax.axis_size("row")
    first_row = lax.axis_index("row") * own_rows - HALO
    local_sum = jnp.sum(spectra, axis=0, dtype=jnp.float32)
    common = lax.psum(local_sum, "row") / channels
    raw_band = padded(spectra, (("row", 0),), HALO)
    band_rows = whiten(raw_band, common)
    lag_matrix = build_table(FREQ, LAGS)
    norm_factor = 1.0 / math.sqrt(FREQ * WIN)
    tile_count = pair_channels.shape[0]
    tile_pairs = pair_channels.shape[1]
    group_count = tile_count // 4
    group_rows = 4 * tile_pairs
    pair_index = (pair_channels - first_row).reshape(group_count, group_rows, 2)
    weights = pair_live.astype(jnp.float32).reshape(group_count, group_rows)

    def correlate(index_rows, weight_rows):
        products = cross_rows(band_rows[index_rows[:, 0]], band_rows[index_rows[:, 1]])
        summed = jnp.dot(products, lag_matrix, preferred_element_type=jnp.float32)
        return summed * norm_factor * weight_rows[:, None]

    def one_group(operands):
        index_rows, weight_rows = operands
        outcome = correlate(index_rows, weight_rows)
        return outcome

    result = lax.map(one_group, (pair_index, weights))
    return result.reshape(tile_count, tile_pairs, LAGS)


def solution(mesh):
    placed = (P(("day", "row"), None, None, None), P("row", None, None), P("row", None))
    return jax.shard_map(
        body, mesh=mesh, in_specs=placed, out_specs=P(("day", "row"), None, None), check_vma=False
    )
```

profile of v0, /device:TPU:8, one launch (start us, length us, event | category | flops | bytes accessed | tf_op | source)
XLA Modules:
  0.0 495.4 jit_solution(6996535282205614045)
XLA Ops:
  6.5 7.1 %copy.11 = bf16[128,2,2,4096]{3,0,2,1:T(8,128)(2,1)} copy(bf16[128,2,2,4096]{3,2,1,0:T(2,128)(2,1)} %param.3) | data formatting | bytes 8388608 | tf_op args[0]
  13.6 1.9 collective-permute-start
  15.6 4.5 collective-permute-start.1
  20.1 6.4 %convert_reduce_fusion = f32[2,2,4096]{2,1,0:T(2,128)} fusion(bf16[128,2,2,4096]{3,2,1,0:T(2,128)(2,1)} %param.3), kind=kLoop, calls=%fused_computation.27 | loop fusion | flops 4177920 | bytes 4259840 | tf_op jit(solution)/shard_map/reduce_sum | solution.py:64
  26.5 0.0 all-reduce.2.cloned.1.call-update
  26.6 35.2 %cosine_convert_fusion = (bf16[4096,512]{1,0:T(8,128)(2,1)}, bf16[4096,512]{1,0:T(8,128)(2,1)}) fusion(s32[512]{0:T(512)S(1)} %iota_add_fusion), kind=kLoop, calls=%fused_computation.24 | loop fusion | flops 35651584 | bytes 8390656 | tf_op jit(solution)/shard_map/convert
  61.8 84.3 %all-reduce.2.cloned.1.call-done = f32[2,2,4096]{2,1,0:T(2,128)} async-done(((f32[2,2,4096]{2,1,0:T(2,128)}), f32[2,2,4096]{2,1,0:T(2,128)}) %all-reduce.2.cloned.1.call-update) | async-done | bytes 65552 | tf_op jit(solution)/shard_map/psum | solution.py:65
  146.2 0.9 broadcast_multiply_fusion
  147.0 0.0 collective-permute-done
  147.0 0.0 collective-permute-done.1
  147.1 7.4 %convert_subtract_fusion = f32[384,2,2,4096]{3,0,2,1:T(8,128)S(1)} fusion(bf16[128,2,2,4096]{3,0,2,1:T(8,128)(2,1)} %collective-permute-done.1, bf16[128,2,2,4096]{3,0,2,1:T(8,128)(2,1)} %copy.11, bf16[128,2,2,4096]{3,0,2,1:T(8,128)(2,1)} %collective-permute-done, f32[2,2,4096]{2,1,0:T(2,128)S(1)} %broadcast_multiply_fusion), kind=kLoop, calls=%fused_computation.3 | loop fusion | flops 44040192 | bytes 37814272 | tf_op jit(solution)/shard_map/sub | solution.py:36
  154.5 6.7 %fusion.1 = f32[384,2,1,4096]{3,0,2,1:T(8,128)} fusion(f32[384,2,2,4096]{3,0,2,1:T(8,128)S(1)} %convert_subtract_fusion), kind=kLoop, calls=%fused_computation.8 | loop fusion | flops 9437184 | bytes 37748736 | tf_op jit(solution)/shard_map/sqrt | solution.py:37
  161.2 12.6 %copy.14 = f32[384,2,1,4096]{0,3,1,2:T(8,128)} copy(f32[384,2,1,4096]{3,0,2,1:T(8,128)} %fusion.1) | data formatting | bytes 25165824 | tf_op jit(solution)/shard_map/sqrt | solution.py:37
  173.8 6.4 %reduce_sum.39 = f32[384,2,64]{0,2,1:T(8,128)S(1)} reduce(f32[384,2,64,64]{0,3,2,1:T(8,128)} %bitcast.9, f32[]{:T(128)} %constant.25.clone.1), dimensions={3}, to_apply=%region_2.0 | reduce | flops 3096576 | bytes 12779524 | tf_op jit(solution)/shard_map/reduce_sum | solution.py:40
  180.3 5.3 %div.29 = f32[384,2,64,64]{0,3,2,1:T(8,128)} broadcast(f32[384,2,64]{0,2,1:T(8,128)S(1)} %multiply_add_fusion), dimensions={0,1,2} | broadcast | bytes 12779520 | tf_op jit(solution)/shard_map/div | solution.py:42
  185.5 12.6 %copy.15 = f32[384,2,4096]{2,0,1:T(8,128)} copy(f32[384,2,4096]{0,2,1:T(8,128)} %bitcast.10) | data formatting | bytes 25165824 | tf_op jit(solution)/shard_map/div | solution.py:42
  198.2 10.2 %divide_convert_fusion = bf16[384,2,2,4096]{3,0,2,1:T(8,128)(2,1)S(1)} fusion(f32[384,2,4096]{2,0,1:T(8,128)} %copy.15, f32[2,2,4096]{2,1,0:T(2,128)S(1)} %broadcast_multiply_fusion, bf16[128,2,2,4096]{3,0,2,1:T(8,128)(2,1)} %collective-permute-done.1, bf16[128,2,2,4096]{3,0,2,1:T(8,128)(2,1)} %copy.11, bf16[128,2,2,4096]{3,0,2,1:T(8,128)(2,1)} %collective-permute-done), kind=kLoop, calls=%fused_computation.2 | loop fusion | flops 56623104 | bytes 37814272 | tf_op jit(solution)/shard_map/convert_element_type | solution.py:45
  208.4 30.0 %copy.17 = bf16[384,2,2,4096]{3,2,1,0:T(2,128)(2,1)} copy(bf16[384,2,2,4096]{3,0,2,1:T(8,128)(2,1)S(1)} %divide_convert_fusion) | data formatting | bytes 25165824 | tf_op jit(solution)/shard_map/convert_element_type | solution.py:45
  238.3 47.0 %gather_fusion = bf16[512,2,2,4096]{3,2,1,0:T(2,128)(2,1)} fusion(bf16[384,2,2,4096]{3,2,1,0:T(2,128)(2,1)} %copy.17, s32[1024]{0:T(1024)S(1)} %pad_clamp_fusion.1), kind=kCustom, calls=%fused_computation | custom fusion | bytes 33556480 | tf_op jit(solution)/shard_map/while/body/eval_jaxpr/gather | solution.py:78
  285.4 17.6 %convert_element_type.33 = f32[512,2,2,4096]{3,2,1,0:T(2,128)} convert(bf16[512,2,2,4096]{3,2,1,0:T(2,128)(2,1)} %gather_fusion) | non-fusion elementwise | flops 8388608 | bytes 50331648 | tf_op jit(solution)/shard_map/while/body/eval_jaxpr/convert_element_type | solution.py:49
  303.0 46.8 %gather_fusion.1 = bf16[512,2,2,4096]{3,2,1,0:T(2,128)(2,1)} fusion(bf16[384,2,2,4096]{3,2,1,0:T(2,128)(2,1)} %copy.17, s32[1024]{0:T(1024)S(1)} %pad_clamp_fusion), kind=kCustom, calls=%fused_computation.1 | custom fusion | bytes 33556480 | tf_op jit(solution)/shard_map/while/body/eval_jaxpr/gather | solution.py:78
  349.8 17.6 %convert_element_type.34 = f32[512,2,2,4096]{3,2,1,0:T(2,128)} convert(bf16[512,2,2,4096]{3,2,1,0:T(2,128)(2,1)} %gather_fusion.1) | non-fusion elementwise | flops 8388608 | bytes 50331648 | tf_op jit(solution)/shard_map/while/body/eval_jaxpr/convert_element_type | solution.py:50
  367.4 113.5 %add_reduce_fusion = (bf16[512,4096]{1,0:T(8,128)(2,1)S(1)}, bf16[512,4096]{1,0:T(8,128)(2,1)S(1)}) fusion(f32[512,2,2,4096]{3,2,1,0:T(2,128)} %convert_element_type.34, f32[512,2,2,4096]{3,2,1,0:T(2,128)} %convert_element_type.33), kind=kLoop, calls=%fused_computation.5 | loop fusion | flops 29360128 | bytes 75497472 | tf_op jit(solution)/shard_map/while/body/eval_jaxpr/reduce_sum | solution.py:51
  480.9 7.6 %fusion.15 = f32[512,512]{1,0:T(8,128)} fusion(bf16[4096,512]{1,0:T(8,128)(2,1)} %get-tuple-element.28, bf16[4096,512]{1,0:T(8,128)(2,1)S(1)} %copy-done, bf16[512,4096]{1,0:T(8,128)(2,1)S(1)} %get-tuple-element.16, bf16[512,4096]{1,0:T(8,128)(2,1)S(1)} %get-tuple-element.15, f32[512]{0:T(512)S(1)} %multiply_bitcast_fusion), kind=kOutput, calls=%fused_computation.29 | convolution fusion | flops 4328783872 | bytes 17827840 | tf_op jit(solution)/shard_map/while/body/eval_jaxpr/dot_general | solution.py:79
  (14 shorter events, 0.1 us)
Async XLA Ops:
  6.5 20.0 %copy-start.1 = (s32[4,128,2]{1,2,0:T(2,128)S(1)}, s32[4,128,2]{1,2,0:T(2,128)}, u32[]{:S(2)}) copy-start(s32[4,128,2]{1,2,0:T(2,128)} %param.4) | copy-start | bytes 12292
  6.5 20.0 %copy-start.2 = (s32[4,128]{1,0:T(4,128)S(1)}, s32[4,128]{1,0:T(4,128)}, u32[]{:S(2)}) copy-start(s32[4,128]{1,0:T(4,128)} %param.5) | copy-start | bytes 6148
  6.5 139.6 %all-reduce.2.cloned.1.call-start = ((), (), s32[]{:S(2)}) async-start(), calls=%async_computation | async-start | bytes 131072 | tf_op jit(solution)/shard_map/psum | solution.py:65
  13.6 133.4 %collective-permute-start = (bf16[128,2,2,4096]{3,0,2,1:T(8,128)(2,1)}, bf16[128,2,2,4096]{3,0,2,1:T(8,128)(2,1)}, u32[]{:S(2)}, u32[]{:S(2)}) collective-permute-start(bf16[128,2,2,4096]{3,0,2,1:T(8,128)(2,1)} %copy.11), channel_id=1, source_target_pairs={{0,1},{1,2},{2,3},{3,4},{4,5},{5,6},{6,7},{7,8},{8,9},{9,10},{10,1... | collective-permute-start | bytes 12582920 | tf_op jit(solution)/shard_map/ppermute | solution.py:19
  15.6 131.5 %collective-permute-start.1 = (bf16[128,2,2,4096]{3,0,2,1:T(8,128)(2,1)}, bf16[128,2,2,4096]{3,0,2,1:T(8,128)(2,1)}, u32[]{:S(2)}, u32[]{:S(2)}) collective-permute-start(bf16[128,2,2,4096]{3,0,2,1:T(8,128)(2,1)} %copy.11), channel_id=1, source_target_pairs={{1,0},{2,1},{3,2},{4,3},{5,4},{6,5},{7,6},{8,7},{9,8},{10,9},{11,1... | collective-permute-start | bytes 12582920 | tf_op jit(solution)/shard_map/ppermute | solution.py:22
  367.4 113.5 %copy-start = (bf16[4096,512]{1,0:T(8,128)(2,1)S(1)}, bf16[4096,512]{1,0:T(8,128)(2,1)}, u32[]{:S(2)}) copy-start(bf16[4096,512]{1,0:T(8,128)(2,1)} %get-tuple-element.26) | copy-start | bytes 12582916
Sparse Core Ops, SparseCore 0:
  26.6 119.4 all-reduce.1
where the time goes:
time: 497 us; the launch traced here: 495 us
  other arithmetic  222 us (45%)
  local copies, waits for them, and re-layouts  161 us (32%)
  waiting for transfers between devices  84.4 us (17%)
  between operations  13.5 us (3%)
  matrix products  7.65 us (2%)
  starting transfers between devices  6.45 us (1%)
    reduce_sum x1, other arithmetic, cross_rows(): jnp.sum(first_f32[:, :, 0] * second_f32[:, :, 0] + first_f32[:, :, 1] * s...  114 us
    psum x1, waiting for transfers between devices, body(): common = lax.psum(local_sum, 'row') / channels  84.3 us
    gather x1, local copies, waits for them, and re-layouts, correlate(): band_rows[index_rows[:, 0]]  47 us
    gather x1, local copies, waits for them, and re-layouts, correlate(): band_rows[index_rows[:, 1]]  46.8 us
    another operation x1, other arithmetic  35.2 us
    convert_element_type x1, local copies, waits for them, and re-layouts, whiten(): return scaled.reshape(raw_rows.shape).astype(jnp.bfloat16)  30 us
    div x2, local copies, waits for them, and re-layouts, whiten(): removed.reshape(row_count, window_count, 2, bin_count // BAND, BAND)  17.9 us
    convert_element_type x1, other arithmetic, cross_rows(): first_f32 = first_rows.astype(jnp.float32)  17.6 us
  transfers between devices with their start and end apart: 3, of which 1 were waited for; matrix products, arithmetic and copies ran while one was open for 9% of the time, Pallas kernels for 0%

commit v1 on v0

--- a/solution.py
+++ b/solution.py
@@ -9,6 +9,12 @@
 BAND = 64
 LAGS = 512
 HALO = 128
+
+
+def gather_and_add(shard, name):
+    parts = lax.all_gather(shard, name, axis=0, tiled=False)
+    total = parts.sum(axis=0)
+    return total
 
 
 def padded(block, sides, width):
@@ -62,7 +68,7 @@
     channels = own_rows * lax.axis_size("row")
     first_row = lax.axis_index("row") * own_rows - HALO
     local_sum = jnp.sum(spectra, axis=0, dtype=jnp.float32)
-    common = lax.psum(local_sum, "row") / channels
+    common = gather_and_add(local_sum, "row") / channels
     raw_band = padded(spectra, (("row", 0),), HALO)
     band_rows = whiten(raw_band, common)
     lag_matrix = build_table(FREQ, LAGS)

time: 497 us -> 463 us (0.932)
  the two profiles are of different devices: /device:TPU:8 before, /device:TPU:25 now
where the time goes in v1:
time: 463 us; the launch traced here: 461 us
  other arithmetic  223 us (48%)
  local copies, waits for them, and re-layouts  161 us (35%)
  waiting for transfers between devices  50.5 us (11%)
  between operations  13.5 us (3%)
  matrix products  7.64 us (2%)
  starting transfers between devices  5.62 us (1%)
    reduce_sum x1, other arithmetic, cross_rows(): jnp.sum(first_f32[:, :, 0] * second_f32[:, :, 0] + first_f32[:, :, 1] * s...  114 us
    gather x1, local copies, waits for them, and re-layouts, correlate(): band_rows[index_rows[:, 0]]  47 us
    gather x1, local copies, waits for them, and re-layouts, correlate(): band_rows[index_rows[:, 1]]  46.8 us
    another operation x1, other arithmetic  35.2 us
    ppermute x1, waiting for transfers between devices, padded(): lax.ppermute(lax.slice_in_dim(block, 0, width, axis=dim), axis, backward)  32.6 us
    convert_element_type x1, local copies, waits for them, and re-layouts, whiten(): return scaled.reshape(raw_rows.shape).astype(jnp.bfloat16)  30 us
    div x2, local copies, waits for them, and re-layouts, whiten(): removed.reshape(row_count, window_count, 2, bin_count // BAND, BAND)  17.9 us
    all_gather x1, waiting for transfers between devices, gather_and_add(): parts = lax.all_gather(shard, name, axis=0, tiled=False)  17.8 us
  transfers between devices with their start and end apart: 3, of which 2 were waited for; matrix products, arithmetic and copies ran while one was open for 9% of the time, Pallas kernels for 0%

profile of v1, /device:TPU:25, one launch (start us, length us, event | category | flops | bytes accessed | tf_op | source)
XLA Modules:
  0.0 461.4 jit_solution(1477528875200243284)
XLA Ops:
  6.5 7.1 %copy.14 = bf16[128,2,2,4096]{3,0,2,1:T(8,128)(2,1)} copy(bf16[128,2,2,4096]{3,2,1,0:T(2,128)(2,1)} %param.3) | data formatting | bytes 8388608 | tf_op args[0]
  13.6 3.7 collective-permute-start
  17.3 1.9 collective-permute-start.1
  19.3 6.4 %convert_reduce_fusion = f32[2,2,4096]{2,1,0:T(2,128)} fusion(bf16[128,2,2,4096]{3,2,1,0:T(2,128)(2,1)} %param.3), kind=kLoop, calls=%fused_computation.27 | loop fusion | flops 4177920 | bytes 4259840 | tf_op jit(solution)/shard_map/reduce_sum | solution.py:70
  25.6 0.0 all-gather.3.cloned.1.call-update
  25.8 35.2 %cosine_convert_fusion = (bf16[4096,512]{1,0:T(8,128)(2,1)}, bf16[4096,512]{1,0:T(8,128)(2,1)}) fusion(s32[512]{0:T(512)S(1)} %iota_add_fusion), kind=kLoop, calls=%fused_computation.24 | loop fusion | flops 35651584 | bytes 8390656 | tf_op jit(solution)/shard_map/convert
  61.0 17.8 %all-gather.3.cloned.1.call-done = f32[32,2,4096]{2,1,0:T(2,128)} async-done(((f32[2,2,4096]{2,1,0:T(2,128)}), f32[32,2,4096]{2,1,0:T(2,128)}) %all-gather.3.cloned.1.call-update) | async-done | bytes 1048592 | tf_op jit(solution)/shard_map/all_gather | solution.py:15
  78.8 1.6 reduce_sum.48
  80.5 0.0 collective-permute-done
  80.5 32.6 %collective-permute-done.1 = bf16[128,2,2,4096]{3,0,2,1:T(8,128)(2,1)} collective-permute-done((bf16[128,2,2,4096]{3,0,2,1:T(8,128)(2,1)}, bf16[128,2,2,4096]{3,0,2,1:T(8,128)(2,1)}, u32[]{:S(2)}, u32[]{:S(2)}) %collective-permute-start.1) | collective-permute-done | bytes 4194336 | tf_op jit(solution)/shard_map/ppermute | solution.py:28
  113.1 7.4 %convert_subtract_fusion = f32[384,2,2,4096]{3,0,2,1:T(8,128)S(1)} fusion(bf16[128,2,2,4096]{3,0,2,1:T(8,128)(2,1)} %collective-permute-done.1, bf16[128,2,2,4096]{3,0,2,1:T(8,128)(2,1)} %copy.14, bf16[128,2,2,4096]{3,0,2,1:T(8,128)(2,1)} %collective-permute-done, f32[2,2,4096]{2,1,0:T(2,128)S(1)} %broadcast_multiply_fusion), kind=kLoop, calls=%fused_computation.3 | loop fusion | flops 44040192 | bytes 37814272 | tf_op jit(solution)/shard_map/sub | solution.py:42
  120.5 6.7 %fusion.1 = f32[384,2,1,4096]{3,0,2,1:T(8,128)} fusion(f32[384,2,2,4096]{3,0,2,1:T(8,128)S(1)} %convert_subtract_fusion), kind=kLoop, calls=%fused_computation.8 | loop fusion | flops 9437184 | bytes 37748736 | tf_op jit(solution)/shard_map/sqrt | solution.py:43
  127.2 12.6 %copy.17 = f32[384,2,1,4096]{0,3,1,2:T(8,128)} copy(f32[384,2,1,4096]{3,0,2,1:T(8,128)} %fusion.1) | data formatting | bytes 25165824 | tf_op jit(solution)/shard_map/sqrt | solution.py:43
  139.8 6.4 %reduce_sum.49 = f32[384,2,64]{0,2,1:T(8,128)S(1)} reduce(f32[384,2,64,64]{0,3,2,1:T(8,128)} %bitcast.10, f32[]{:T(128)} %constant.25.clone.1), dimensions={3}, to_apply=%region_2.0 | reduce | flops 3096576 | bytes 12779524 | tf_op jit(solution)/shard_map/reduce_sum | solution.py:46
  146.3 5.3 %div.29 = f32[384,2,64,64]{0,3,2,1:T(8,128)} broadcast(f32[384,2,64]{0,2,1:T(8,128)S(1)} %multiply_add_fusion), dimensions={0,1,2} | broadcast | bytes 12779520 | tf_op jit(solution)/shard_map/div | solution.py:48
  151.6 12.6 %copy.18 = f32[384,2,4096]{2,0,1:T(8,128)} copy(f32[384,2,4096]{0,2,1:T(8,128)} %bitcast.11) | data formatting | bytes 25165824 | tf_op jit(solution)/shard_map/div | solution.py:48
  164.2 10.2 %divide_convert_fusion = bf16[384,2,2,4096]{3,0,2,1:T(8,128)(2,1)S(1)} fusion(f32[384,2,4096]{2,0,1:T(8,128)} %copy.18, f32[2,2,4096]{2,1,0:T(2,128)S(1)} %broadcast_multiply_fusion, bf16[128,2,2,4096]{3,0,2,1:T(8,128)(2,1)} %collective-permute-done.1, bf16[128,2,2,4096]{3,0,2,1:T(8,128)(2,1)} %copy.14, bf16[128,2,2,4096]{3,0,2,1:T(8,128)(2,1)} %collective-permute-done), kind=kLoop, calls=%fused_computation.2 | loop fusion | flops 56623104 | bytes 37814272 | tf_op jit(solution)/shard_map/convert_element_type | solution.py:51
  174.4 30.0 %copy.20 = bf16[384,2,2,4096]{3,2,1,0:T(2,128)(2,1)} copy(bf16[384,2,2,4096]{3,0,2,1:T(8,128)(2,1)S(1)} %divide_convert_fusion) | data formatting | bytes 25165824 | tf_op jit(solution)/shard_map/convert_element_type | solution.py:51
  204.3 47.0 %gather_fusion = bf16[512,2,2,4096]{3,2,1,0:T(2,128)(2,1)} fusion(bf16[384,2,2,4096]{3,2,1,0:T(2,128)(2,1)} %copy.20, s32[1024]{0:T(1024)S(1)} %pad_clamp_fusion.1), kind=kCustom, calls=%fused_computation | custom fusion | bytes 33556480 | tf_op jit(solution)/shard_map/while/body/eval_jaxpr/gather | solution.py:84
  251.4 17.6 %convert_element_type.33 = f32[512,2,2,4096]{3,2,1,0:T(2,128)} convert(bf16[512,2,2,4096]{3,2,1,0:T(2,128)(2,1)} %gather_fusion) | non-fusion elementwise | flops 8388608 | bytes 50331648 | tf_op jit(solution)/shard_map/while/body/eval_jaxpr/convert_element_type | solution.py:55
  269.0 46.8 %gather_fusion.1 = bf16[512,2,2,4096]{3,2,1,0:T(2,128)(2,1)} fusion(bf16[384,2,2,4096]{3,2,1,0:T(2,128)(2,1)} %copy.20, s32[1024]{0:T(1024)S(1)} %pad_clamp_fusion), kind=kCustom, calls=%fused_computation.1 | custom fusion | bytes 33556480 | tf_op jit(solution)/shard_map/while/body/eval_jaxpr/gather | solution.py:84
  315.8 17.6 %convert_element_type.34 = f32[512,2,2,4096]{3,2,1,0:T(2,128)} convert(bf16[512,2,2,4096]{3,2,1,0:T(2,128)(2,1)} %gather_fusion.1) | non-fusion elementwise | flops 8388608 | bytes 50331648 | tf_op jit(solution)/shard_map/while/body/eval_jaxpr/convert_element_type | solution.py:56
  333.4 113.5 %add_reduce_fusion = (bf16[512,4096]{1,0:T(8,128)(2,1)S(1)}, bf16[512,4096]{1,0:T(8,128)(2,1)S(1)}) fusion(f32[512,2,2,4096]{3,2,1,0:T(2,128)} %convert_element_type.34, f32[512,2,2,4096]{3,2,1,0:T(2,128)} %convert_element_type.33), kind=kLoop, calls=%fused_computation.5 | loop fusion | flops 29360128 | bytes 75497472 | tf_op jit(solution)/shard_map/while/body/eval_jaxpr/reduce_sum | solution.py:57
  446.9 7.6 %fusion.15 = f32[512,512]{1,0:T(8,128)} fusion(bf16[4096,512]{1,0:T(8,128)(2,1)} %get-tuple-element.28, bf16[4096,512]{1,0:T(8,128)(2,1)S(1)} %copy-done, bf16[512,4096]{1,0:T(8,128)(2,1)S(1)} %get-tuple-element.16, bf16[512,4096]{1,0:T(8,128)(2,1)S(1)} %get-tuple-element.15, f32[512]{0:T(512)S(1)} %multiply_bitcast_fusion), kind=kOutput, calls=%fused_computation.29 | convolution fusion | flops 4328783872 | bytes 17827840 | tf_op jit(solution)/shard_map/while/body/eval_jaxpr/dot_general | solution.py:85
  (15 shorter events, 0.1 us)
Async XLA Ops:
  6.5 19.1 %copy-start.1 = (s32[4,128,2]{1,2,0:T(2,128)S(1)}, s32[4,128,2]{1,2,0:T(2,128)}, u32[]{:S(2)}) copy-start(s32[4,128,2]{1,2,0:T(2,128)} %param.4) | copy-start | bytes 12292
  6.5 19.2 %copy-start.2 = (s32[4,128]{1,0:T(4,128)S(1)}, s32[4,128]{1,0:T(4,128)}, u32[]{:S(2)}) copy-start(s32[4,128]{1,0:T(4,128)} %param.5) | copy-start | bytes 6148
  6.5 72.3 %all-gather.3.cloned.1.call-start = ((), (), s32[]{:S(2)}) async-start(), calls=%async_computation | async-start | bytes 1114112 | tf_op jit(solution)/shard_map/all_gather | solution.py:15
  13.6 66.9 %collective-permute-start = (bf16[128,2,2,4096]{3,0,2,1:T(8,128)(2,1)}, bf16[128,2,2,4096]{3,0,2,1:T(8,128)(2,1)}, u32[]{:S(2)}, u32[]{:S(2)}) collective-permute-start(bf16[128,2,2,4096]{3,0,2,1:T(8,128)(2,1)} %copy.14), channel_id=1, source_target_pairs={{0,1},{1,2},{2,3},{3,4},{4,5},{5,6},{6,7},{7,8},{8,9},{9,10},{10,1... | collective-permute-start | bytes 12582920 | tf_op jit(solution)/shard_map/ppermute | solution.py:25
  17.3 95.8 %collective-permute-start.1 = (bf16[128,2,2,4096]{3,0,2,1:T(8,128)(2,1)}, bf16[128,2,2,4096]{3,0,2,1:T(8,128)(2,1)}, u32[]{:S(2)}, u32[]{:S(2)}) collective-permute-start(bf16[128,2,2,4096]{3,0,2,1:T(8,128)(2,1)} %copy.14), channel_id=1, source_target_pairs={{1,0},{2,1},{3,2},{4,3},{5,4},{6,5},{7,6},{8,7},{9,8},{10,9},{11,1... | collective-permute-start | bytes 12582920 | tf_op jit(solution)/shard_map/ppermute | solution.py:28
  333.4 113.5 %copy-start = (bf16[4096,512]{1,0:T(8,128)(2,1)S(1)}, bf16[4096,512]{1,0:T(8,128)(2,1)}, u32[]{:S(2)}) copy-start(bf16[4096,512]{1,0:T(8,128)(2,1)} %get-tuple-element.26) | copy-start | bytes 12582916
Sparse Core Ops, SparseCore 0:
  25.8 53.0 all-gather.2
